TPU v7x, 32 devices: a whole 2x2x4 slice. The times are simulated.
32 devices in a mesh: row: 8 (over z, x), col: 4 (over y, core).
Axes of the slice: x: 2, y: 2, z: 4, core: 2. Of those that a mesh axis runs over, the one named last changes fastest.
Arguments:
- sources_in: bfloat16 [32768, 2, 512], P(('row', 'col')), may hold values from -6 to 6
- right_bases: bfloat16 [64, 8, 2, 96, 512], P(('row', 'col')), may hold values from -0.1875 to 0.1875
- left_bases: bfloat16 [8, 8, 8, 2, 96, 512], P('row', None, 'col'), may hold values from -0.046875 to 0.046875
- tile_ranks: int32 [8, 64], P(None, ('row', 'col')), may hold values from 16 to 96
Outputs:
- redatumed: bfloat16 [4096, 2, 512], P(('row', 'col'))
Inputs may be any that keep to these rules, and one draw needn't show every extreme that they name: `tile_ranks`: each tile's rank; rows of its bases at or beyond it do not count.
All inputs are finite; a program needn't handle non-finite values.
Results may differ from a plain program's by a relative error of at most 0.0049.
Values may be sent and summed in bfloat16 or wider, within the bound.
A program may use at most 256 MiB of HBM per device.

v0:
```python
import jax
import jax.numpy as jnp
from jax import lax
from jax.sharding import PartitionSpec as P


def complex_rows(prod):
    real = prod[:, 0, 0] - prod[:, 1, 1]
    imag = prod[:, 0, 1] + prod[:, 1, 0]
    return jnp.stack([real, imag], 1)


def body(sources_in, right_bases, left_bases, tile_ranks):
    cols, tile_rows, _, rank_pad, width = right_bases.shape
    samples = sources_in.shape[2]
    blocks = sources_in.reshape(cols, width, 2, samples)
    prod = jnp.einsum("cmprb,cbqs->cmpqrs", right_bases, blocks, preferred_element_type=jnp.float32)
    real = prod[:, :, 0, 0] - prod[:, :, 1, 1]
    imag = prod[:, :, 0, 1] + prod[:, :, 1, 0]
    levels = lax.broadcasted_iota(jnp.int32, (cols, tile_rows, rank_pad), 2)
    keep = (levels < tile_ranks.T[:, :, None]).astype(jnp.float32)
    coeffs = (jnp.stack([real, imag], 2) * keep[:, :, None, :, None]).astype(jnp.bfloat16)
    left_flat = left_bases.reshape(-1, 2, rank_pad, width)
    picked = lax.all_to_all(coeffs, "row", split_axis=1, concat_axis=0, tiled=True)[:, 0]
    terms = jnp.einsum("jpkb,jqks->bpqs", left_flat, picked, preferred_element_type=jnp.float32)
    partial_value = complex_rows(terms)
    return lax.psum_scatter(partial_value, "col", scatter_dimension=0, tiled=True).astype(
        jnp.bfloat16
    )


def solution(mesh):
    in_specs = (
        P(("row", "col"), None, None),
        P(("row", "col"), None, None, None, None),
        P("row", None, "col", None, None, None),
        P(None, ("row", "col")),
    )
    out_specs = P(("row", "col"), None, None)
    return jax.shard_map(body, mesh=mesh, in_specs=in_specs, out_specs=out_specs, check_vma=False)
```

profile of v0, /device:TPU:0, one launch (start us, length us, event | category | flops | bytes accessed | tf_op | source)
XLA Modules:
  0.0 140.6 jit_solution(18144170342708530463)
XLA Ops:
  6.5 0.0 copy-start
  6.5 0.0 reduce-scatter.2.cloned.1.call-start
  6.5 1.9 %copy-done = bf16[2,8,2,96,512]{4,3,2,1,0:T(8,128)(2,1)S(1)} copy-done((bf16[2,8,2,96,512]{4,3,2,1,0:T(8,128)(2,1)S(1)}, bf16[2,8,2,96,512]{4,3,2,1,0:T(8,128)(2,1)}, u32[]{:S(2)}) %copy-start) | copy-done | bytes 3145752
  8.4 5.0 %convolution_bitcast_fusion = f32[2,8,2,2,96,512]{5,4,2,1,3,0:T(8,128)S(1)} fusion(bf16[2,8,2,96,512]{4,3,2,1,0:T(8,128)(2,1)S(1)} %copy-done, bf16[2,512,2,512,1,1]{3,2,1,0,5,4:T(2,128)(2,1)} %bitcast.60), kind=kOutput, calls=%fused_computation.2 | convolution fusion | flops 3221225472 | bytes 17825792 | tf_op jit(solution)/shard_map/cmprb,cbqs->cmpqrs/dot_general | solution.py:17
  13.4 0.9 fusion.1
  14.3 0.0 copy-start.1
  14.3 0.9 fusion.3
  15.2 0.0 copy-done.1
  15.2 0.1 fusion.18
  15.3 0.5 fusion
  15.8 0.3 copy.24
  16.1 77.8 %all_to_all.15 = bf16[2,8,2,96,512]{4,3,0,2,1:T(8,128)(2,1)S(1)} all-to-all(bf16[2,8,2,96,512]{4,3,0,2,1:T(8,128)(2,1)S(1)} %copy.24), channel_id=1, replica_groups=mesh['row'=8,'col'=4] {'row'}, dimensions={1} | all-to-all | bytes 6291456 | tf_op jit(solution)/shard_map/all_to_all | solution.py:24
  93.9 0.0 copy-start.2
  93.9 0.3 copy.25
  94.2 1.6 %copy-done.2 = bf16[1,8,2,2,96,512]{5,4,3,2,1,0:T(8,128)(2,1)S(1)} copy-done((bf16[1,8,2,2,96,512]{5,4,3,2,1,0:T(8,128)(2,1)S(1)}, bf16[1,8,2,2,96,512]{5,4,3,2,1,0:T(8,128)(2,1)}, u32[]{:S(2)}) %copy-start.2) | copy-done | bytes 3145752
  95.8 3.5 %fusion.9 = f32[512,2,2,512]{0,3,1,2:T(8,128)S(1)} fusion(bf16[16,2,96,512]{3,2,1,0:T(8,128)(2,1)S(1)} %bitcast.59, bf16[16,2,96,512,1]{3,2,1,0,4:T(8,128)(2,1)S(1)} %bitcast.57), kind=kOutput, calls=%fused_computation.14 | convolution fusion | flops 3221225472 | bytes 10485760 | tf_op jit(solution)/shard_map/jpkb,jqks->bpqs/dot_general | solution.py:25
  99.2 0.2 fusion.15
  99.4 0.2 fusion.17
  99.7 1.5 %pad_maximum_fusion = f32[512,2,512]{0,2,1:T(8,128)} fusion(f32[512,1,512]{0,2,1:T(8,128)S(1)} %fusion.15, f32[512,1,512]{0,2,1:T(8,128)S(1)} %fusion.17), kind=kLoop, calls=%fused_computation.15 | loop fusion | flops 524288 | bytes 4194304 | tf_op jit(solution)/shard_map/stack | solution.py:10
  101.2 0.0 reduce-scatter.2.cloned.1.call-update
  101.2 30.6 %reduce-scatter.2.cloned.1.call-done = f32[128,2,512]{0,2,1:T(8,128)} async-done(((f32[512,2,512]{0,2,1:T(8,128)}), f32[128,2,512]{0,2,1:T(8,128)}) %reduce-scatter.2.cloned.1.call-update) | async-done | bytes 524304 | tf_op jit(solution)/shard_map/reduce_scatter | solution.py:27
  131.8 1.1 convert_element_type.15
  132.9 0.9 copy.30
Async XLA Ops:
  6.5 1.9 %copy-start = (bf16[2,8,2,96,512]{4,3,2,1,0:T(8,128)(2,1)S(1)}, bf16[2,8,2,96,512]{4,3,2,1,0:T(8,128)(2,1)}, u32[]{:S(2)}) copy-start(bf16[2,8,2,96,512]{4,3,2,1,0:T(8,128)(2,1)} %param.5) | copy-start | bytes 9437188
  6.5 125.2 %reduce-scatter.2.cloned.1.call-start = ((), (), s32[]{:S(2)}) async-start(), calls=%async_computation.2 | async-start | bytes 2621440 | tf_op jit(solution)/shard_map/reduce_scatter | solution.py:27
  14.3 0.9 copy-start.1
  93.9 1.9 %copy-start.2 = (bf16[1,8,2,2,96,512]{5,4,3,2,1,0:T(8,128)(2,1)S(1)}, bf16[1,8,2,2,96,512]{5,4,3,2,1,0:T(8,128)(2,1)}, u32[]{:S(2)}) copy-start(bf16[1,8,2,2,96,512]{5,4,3,2,1,0:T(8,128)(2,1)} %param.6) | copy-start | bytes 9437188
Sparse Core Ops, SparseCore 0:
  101.3 30.4 reduce-scatter.1
where the time goes:
time: 141 us
  blocking collectives  77.8 us (55%)
  waiting for transfers between devices  30.6 us (22%)
  between operations  13.5 us (10%)
  matrix products  8.46 us (6%)
  other arithmetic  5.29 us (4%)
  local copies, waits for them, and re-layouts  4.98 us (4%)
    all_to_all x1, blocking collectives, body(): lax.all_to_all(coeffs, 'row', split_axis=1, concat_axis=0, tiled=True)[:, 0]  77.8 us
    reduce_scatter x1, waiting for transfers between devices, body(): lax.psum_scatter(partial_value, 'col', scatter_dimension=0, tiled=True)  30.6 us
    dot_general x1, matrix products, body(): jnp.einsum('cmprb,cbqs->cmpqrs', right_bases, blocks, preferred_element_t...  5 us
    dot_general x1, matrix products, body(): jnp.einsum('jpkb,jqks->bpqs', left_flat, picked, preferred_element_type=j...  3.46 us
    unnamed x6, local copies, waits for them, and re-layouts  3.46 us
  transfers between devices with their start and end apart: 1, of which 1 were waited for; matrix products, arithmetic and copies ran while one was open for 0% of the time, Pallas kernels for 0%

commit v1 on v0

--- a/solution.py
+++ b/solution.py
@@ -2,6 +2,7 @@
 import jax.numpy as jnp
 from jax import lax
 from jax.sharding import PartitionSpec as P
+from jax.lax import all_to_all, axis_size
 
 
 def complex_rows(prod):
@@ -21,7 +22,9 @@
     keep = (levels < tile_ranks.T[:, :, None]).astype(jnp.float32)
     coeffs = (jnp.stack([real, imag], 2) * keep[:, :, None, :, None]).astype(jnp.bfloat16)
     left_flat = left_bases.reshape(-1, 2, rank_pad, width)
-    picked = lax.all_to_all(coeffs, "row", split_axis=1, concat_axis=0, tiled=True)[:, 0]
+    picked = jnp.concatenate(
+        all_to_all(jnp.stack(jnp.split(coeffs, axis_size("row"), 1), 0), "row", 0, 0), 0
+    )[:, 0]
     terms = jnp.einsum("jpkb,jqks->bpqs", left_flat, picked, preferred_element_type=jnp.float32)
     partial_value = complex_rows(terms)
     return lax.psum_scatter(partial_value, "col", scatter_dimension=0, tiled=True).astype(

time: 141 us -> 141 us (level)
    unnamed x6 -> x13, local copies, waits for them, and re-layouts: 3.46 us -> 3.65 us
where the time goes in v1:
time: 141 us
  blocking collectives  77.8 us (55%)
  waiting for transfers between devices  30.6 us (22%)
  between operations  13.5 us (10%)
  matrix products  8.46 us (6%)
  other arithmetic  5.29 us (4%)
  local copies, waits for them, and re-layouts  4.88 us (3%)
    all_to_all x1, blocking collectives, body(): all_to_all(jnp.stack(jnp.split(coeffs, axis_size('row'), 1), 0), 'row', 0...  77.8 us
    reduce_scatter x1, waiting for transfers between devices, body(): lax.psum_scatter(partial_value, 'col', scatter_dimension=0, tiled=True)  30.6 us
    dot_general x1, matrix products, body(): jnp.einsum('cmprb,cbqs->cmpqrs', right_bases, blocks, preferred_element_t...  5 us
    unnamed x13, local copies, waits for them, and re-layouts  3.65 us
    dot_general x1, matrix products, body(): jnp.einsum('jpkb,jqks->bpqs', left_flat, picked, preferred_element_type=j...  3.46 us
  transfers between devices with their start and end apart: 1, of which 1 were waited for; matrix products, arithmetic and copies ran while one was open for 0% of the time, Pallas kernels for 0%

profile of v1, /device:TPU:0, one launch (start us, length us, event | category | flops | bytes accessed | tf_op | source)
XLA Modules:
  0.0 140.5 jit_solution(3118832098388239922)
XLA Ops:
  6.5 0.0 copy-start
  6.5 0.0 reduce-scatter.2.cloned.1.call-start
  6.5 1.9 %copy-done = bf16[2,8,2,96,512]{4,3,2,1,0:T(8,128)(2,1)S(1)} copy-done((bf16[2,8,2,96,512]{4,3,2,1,0:T(8,128)(2,1)S(1)}, bf16[2,8,2,96,512]{4,3,2,1,0:T(8,128)(2,1)}, u32[]{:S(2)}) %copy-start) | copy-done | bytes 3145752
  8.4 5.0 %convolution_bitcast_fusion = f32[2,8,2,2,96,512]{5,4,2,1,3,0:T(8,128)S(1)} fusion(bf16[2,8,2,96,512]{4,3,2,1,0:T(8,128)(2,1)S(1)} %copy-done, bf16[2,512,2,512,1,1]{3,2,1,0,5,4:T(2,128)(2,1)} %bitcast.102), kind=kOutput, calls=%fused_computation.2 | convolution fusion | flops 3221225472 | bytes 17825792 | tf_op jit(solution)/shard_map/cmprb,cbqs->cmpqrs/dot_general | solution.py:18
  13.4 0.9 fusion.1
  14.3 0.0 copy-start.1
  14.3 0.9 fusion.3
  15.2 0.0 copy-done.1
  15.2 0.1 fusion.26
  15.3 0.5 fusion
  16.1 77.8 %all_to_all.5 = bf16[8,2,1,2,96,512]{5,4,1,3,2,0:T(8,128)(2,1)S(1)} all-to-all(bf16[8,2,1,2,96,512]{5,4,1,3,2,0:T(8,128)(2,1)S(1)} %fusion.18), channel_id=1, replica_groups=mesh['row'=8,'col'=4] {'row'}, dimensions={0} | all-to-all | bytes 6291456 | tf_op jit(solution)/shard_map/all_to_all | solution.py:26
  93.8 0.0 copy-start.2
  93.8 0.3 copy.29
  94.1 1.6 %copy-done.2 = bf16[1,8,2,2,96,512]{5,4,3,2,1,0:T(8,128)(2,1)S(1)} copy-done((bf16[1,8,2,2,96,512]{5,4,3,2,1,0:T(8,128)(2,1)S(1)}, bf16[1,8,2,2,96,512]{5,4,3,2,1,0:T(8,128)(2,1)}, u32[]{:S(2)}) %copy-start.2) | copy-done | bytes 3145752
  95.7 3.5 %fusion.9 = f32[512,2,2,512]{0,3,1,2:T(8,128)S(1)} fusion(bf16[16,2,96,512]{3,2,1,0:T(8,128)(2,1)S(1)} %bitcast.101, bf16[16,2,96,512,1]{3,2,1,0,4:T(8,128)(2,1)S(1)} %bitcast.99), kind=kOutput, calls=%fused_computation.14 | convolution fusion | flops 3221225472 | bytes 10485760 | tf_op jit(solution)/shard_map/jpkb,jqks->bpqs/dot_general | solution.py:28
  99.2 0.2 fusion.15
  99.4 0.2 fusion.17
  99.6 1.5 %pad_maximum_fusion = f32[512,2,512]{0,2,1:T(8,128)} fusion(f32[512,1,512]{0,2,1:T(8,128)S(1)} %fusion.15, f32[512,1,512]{0,2,1:T(8,128)S(1)} %fusion.17), kind=kLoop, calls=%fused_computation.15 | loop fusion | flops 524288 | bytes 4194304 | tf_op jit(solution)/shard_map/stack | solution.py:11
  101.1 0.0 reduce-scatter.2.cloned.1.call-update
  101.1 30.6 %reduce-scatter.2.cloned.1.call-done = f32[128,2,512]{0,2,1:T(8,128)} async-done(((f32[512,2,512]{0,2,1:T(8,128)}), f32[128,2,512]{0,2,1:T(8,128)}) %reduce-scatter.2.cloned.1.call-update) | async-done | bytes 524304 | tf_op jit(solution)/shard_map/reduce_scatter | solution.py:30
  131.7 1.1 convert_element_type.15
  132.8 0.9 copy.34
  (8 shorter events, 0.2 us)
Async XLA Ops:
  6.5 1.9 %copy-start = (bf16[2,8,2,96,512]{4,3,2,1,0:T(8,128)(2,1)S(1)}, bf16[2,8,2,96,512]{4,3,2,1,0:T(8,128)(2,1)}, u32[]{:S(2)}) copy-start(bf16[2,8,2,96,512]{4,3,2,1,0:T(8,128)(2,1)} %param.5) | copy-start | bytes 9437188
  6.5 125.2 %reduce-scatter.2.cloned.1.call-start = ((), (), s32[]{:S(2)}) async-start(), calls=%async_computation.2 | async-start | bytes 2621440 | tf_op jit(solution)/shard_map/reduce_scatter | solution.py:30
  14.3 0.9 copy-start.1
  93.8 1.9 %copy-start.2 = (bf16[1,8,2,2,96,512]{5,4,3,2,1,0:T(8,128)(2,1)S(1)}, bf16[1,8,2,2,96,512]{5,4,3,2,1,0:T(8,128)(2,1)}, u32[]{:S(2)}) copy-start(bf16[1,8,2,2,96,512]{5,4,3,2,1,0:T(8,128)(2,1)} %param.6) | copy-start | bytes 9437188
Sparse Core Ops, SparseCore 0:
  101.3 30.4 reduce-scatter.1
